TPU v7x, 256 devices: a whole 4x4x8 slice. The times are simulated.
256 devices in a mesh: row: 32 (over z_hi, y, core), col: 8 (over z_lo, x).
Axes of the slice: x: 4, y: 4, z: 8 (z_hi: 4, z_lo: 2; z = z_hi * 2 + z_lo), core: 2. Of those that a mesh axis runs over, the one named last changes fastest.
Arguments:
- left: float32 [128, 16384], P('col', 'row'), may hold values from -12 to 12
- right: float32 [128, 16384], P('row', 'col'), may hold values from -12 to 12
- w_out: float32 [1024, 128], replicated, may hold values from -0.1875 to 0.1875
- b_out: float32 [128], replicated, may hold values from -3 to 3
- pair_grad: float32 [512, 512, 128], P('row', 'col'), may hold values from -6 to 6
Outputs:
- pair_out: float32 [512, 512, 128], P('row', 'col')
- grad_left: float32 [128, 16384], P('col', 'row')
- grad_right: float32 [128, 16384], P('row', 'col')
- grad_weight: float32 [1024, 128], replicated
- grad_bias: float32 [128], replicated
All inputs are finite; a program needn't handle non-finite values.
Results may differ from a plain program's by a relative error of at most 0.0001.
Values sent between devices are 32-bit elements; how exact they have to be, the bound alone decides.
No kernel may reach another device: no remote copies, remote signals or barrier semaphores. Data moves between devices by JAX's collectives and lax.ppermute only.
A program may use at most 128 MiB of HBM per device.

v0:
```python
import jax
import jax.numpy as jnp
from jax import lax
from jax.sharding import PartitionSpec as P

C = 32
Z = 128
S = 128


def body(left, right, w_out, b_out, pair_grad):
    highest = lax.Precision.HIGHEST
    tile_rows = left.shape[1] // C
    tile_cols = right.shape[1] // C
    residues = tile_rows * lax.axis_size("row")
    weight_cube = w_out.reshape(C, C, Z)
    contract_rows = (((0,), (0,)), ((), ()))
    contract_cols = (((1,), (1,)), ((), ()))
    left_all = lax.all_gather(left, "col", axis=0, tiled=True)
    right_all = lax.all_gather(right, "row", axis=0, tiled=True)
    outer = (
        lax.dot_general(
            left_all,
            right_all,
            contract_rows,
            precision=highest,
            preferred_element_type=jnp.float32,
        )
        / S
    )
    outer_split = outer.reshape(tile_rows, C, tile_cols, C)
    pair_out = jnp.einsum("icje,cez->ijz", outer_split, weight_cube, precision=highest) + b_out
    grad_outer = jnp.einsum("ijz,cez->icje", pair_grad, weight_cube, precision=highest)
    grad_outer = grad_outer.reshape(tile_rows * C, tile_cols * C)
    grad_left = lax.psum_scatter(
        lax.dot_general(
            right_all,
            grad_outer,
            contract_cols,
            precision=highest,
            preferred_element_type=jnp.float32,
        )
        / S,
        "col",
        scatter_dimension=0,
        tiled=True,
    )
    grad_right = lax.psum_scatter(
        jnp.dot(left_all, grad_outer, precision=highest) / S, "row", scatter_dimension=0, tiled=True
    )
    weight_term = jnp.einsum("icje,ijz->cez", outer_split, pair_grad, precision=highest).reshape(
        C * C, Z
    )
    bias_term = jnp.sum(pair_grad, axis=(0, 1))
    grad_weight, grad_bias = lax.psum((weight_term, bias_term), ("row", "col"))
    return (pair_out, grad_left, grad_right, grad_weight / residues, grad_bias / residues)


def solution(mesh):
    placed = (P("col", "row"), P("row", "col"), P(), P(), P("row", "col", None))
    return jax.shard_map(
        body,
        mesh=mesh,
        in_specs=placed,
        out_specs=(P("row", "col", None), P("col", "row"), P("row", "col"), P(), P()),
        check_vma=False,
    )
```

profile of v0, /device:TPU:8, one launch (start us, length us, event | category | flops | bytes accessed | tf_op | source)
XLA Modules:
  0.0 770.1 jit_solution(7213743941106208333)
XLA Ops:
  7.2 29.5 %all_gather.6 = f32[128,512]{1,0:T(8,128)S(1)} all-gather(f32[16,512]{1,0:T(8,128)} %param.5), channel_id=1, replica_groups=mesh['row'=32,'col'=8] {'col'}, dimensions={0}, use_global_device_ids=true | all-gather | bytes 294912 | tf_op jit(solution)/shard_map/all_gather | solution.py:19
  36.8 9.8 %convolution_bitcast_fusion = f32[16,32,64,32]{2,3,0,1:T(8,128)} fusion(f32[32,32,128,1]{2,1,3,0:T(8,128)S(1)} %bitcast.42, f32[16,64,128]{2,1,0:T(8,128)} %param.9), kind=kOutput, calls=%fused_computation.1 | convolution fusion | flops 1610612736 | bytes 5242880 | tf_op jit(solution)/shard_map/ijz,cez->icje/dot_general | solution.py:33
  46.6 12.3 %copy.21 = f32[16,32,64,32]{3,2,1,0:T(8,128)} copy(f32[16,32,64,32]{2,3,0,1:T(8,128)} %convolution_bitcast_fusion) | data formatting | bytes 8388608 | tf_op jit(solution)/shard_map/ijz,cez->icje/transpose | solution.py:33
  58.9 13.5 %reshape.24 = f32[512,2048]{1,0:T(8,128)} reshape(f32[16,32,64,32]{3,2,1,0:T(8,128)} %copy.21) | data formatting | bytes 8388608 | tf_op jit(solution)/shard_map/reshape | solution.py:34
  72.4 9.9 %fusion = f32[128,2048]{0,1:T(8,128)} fusion(f32[512,2048]{1,0:T(8,128)} %reshape.24, f32[128,512]{1,0:T(8,128)S(1)} %all_gather.6), kind=kOutput, calls=%fused_computation.3 | convolution fusion | flops 1610874880 | bytes 5505024 | tf_op jit(solution)/shard_map/dot_general | solution.py:49
  82.3 0.7 all-gather.3.cloned.1.call-update
  83.4 0.6 dynamic-slice
  84.7 77.5 %psum.15 = f32[128]{0:T(128)S(1)} all-reduce(f32[128]{0:T(128)S(1)} %reduce_sum.9), channel_id=1, replica_groups=mesh['row'=32,'col'=8] {'row','col'}, use_global_device_ids=true, to_apply=%region_4.0 | all-reduce | flops 128 | bytes 1024 | tf_op jit(solution)/shard_map/psum | solution.py:55
  162.1 0.5 broadcast_multiply_fusion.1
  162.6 205.9 %all-reduce.6.cloned.1.call-done = f32[128,2048]{0,1:T(8,128)} async-done(((f32[128,2048]{0,1:T(8,128)}), f32[128,2048]{0,1:T(8,128)}) %all-reduce.6.cloned.1.call-update) | async-done | bytes 1048592
  368.6 1.6 constant_dynamic-slice_fusion
  370.1 0.9 copy.25
  371.1 55.6 %all-gather.3.cloned.1.call-done = f32[32,4,2048]{2,1,0:T(4,128)} async-done(((f32[1,4,2048]{2,1,0:T(4,128)}), f32[32,4,2048]{2,1,0:T(4,128)}) %all-gather.3.cloned.1.call-update) | async-done | bytes 1048592 | tf_op jit(solution)/shard_map/all_gather | solution.py:20
  426.7 1.6 reshape.26
  428.3 5.0 convolution_multiply_fusion
  433.3 11.4 %reshape.22 = f32[16,32,64,32]{3,2,1,0:T(8,128)} reshape(f32[512,2048]{1,0:T(8,128)} %convolution_multiply_fusion) | data formatting | bytes 8388608 | tf_op jit(solution)/shard_map/reshape | solution.py:31
  444.7 12.7 %copy.33 = f32[32,32,16,64]{3,1,0,2:T(8,128)} copy(f32[32,32,16,64]{1,3,0,2:T(8,128)} %bitcast.44) | data formatting | bytes 8388608 | tf_op jit(solution)/shard_map/icje,ijz->cez/dot_general | solution.py:51
  457.4 9.9 %convolution_bitcast_fusion.2 = f32[1024,128]{1,0:T(8,128)} fusion(f32[1024,16,64]{2,0,1:T(8,128)} %bitcast.45, f32[16,64,128]{2,1,0:T(8,128)S(1)} %copy-done.1), kind=kOutput, calls=%fused_computation.5 | convolution fusion | flops 1610612736 | bytes 5242880 | tf_op jit(solution)/shard_map/icje,ijz->cez/dot_general | solution.py:51
  467.6 5.2 fusion.2
  472.8 0.8 copy.29
  473.7 17.6 %fusion.1 = f32[16,64,128]{2,1,0:T(8,128)} fusion(f32[16,32,64,32]{3,2,1,0:T(8,128)} %reshape.22, f32[32,32,128,1]{2,1,0,3:T(8,128)S(1)} %bitcast.43, f32[128]{0:T(128)S(1)} %copy-done.2), kind=kOutput, calls=%fused_computation.6 | convolution fusion | flops 1610743808 | bytes 5243392 | tf_op jit(solution)/shard_map/icje,cez->ijz/dot_general | solution.py:32
  491.3 230.2 %all-reduce.4.cloned.1.call-done = f32[1024,128]{1,0:T(8,128)} async-done(((f32[1024,128]{1,0:T(8,128)}), f32[1024,128]{1,0:T(8,128)}) %all-reduce.4.cloned.1.call-update) | async-done | bytes 524304 | tf_op jit(solution)/shard_map/psum | solution.py:55
  721.5 1.9 broadcast_multiply_fusion
  723.4 40.2 %reduce-scatter.5.cloned.1.call-done = f32[16,512]{1,0:T(8,128)} async-done(((f32[128,512]{1,0:T(8,128)}), f32[16,512]{1,0:T(8,128)}) %reduce-scatter.5.cloned.1.call-update) | async-done | bytes 32784
  (16 shorter events, 0.8 us)
Async XLA Ops:
  7.2 29.6 %copy-start = (f32[1024,128]{1,0:T(8,128)S(1)}, f32[1024,128]{1,0:T(8,128)}, u32[]{:S(2)}) copy-start(f32[1024,128]{1,0:T(8,128)} %param.7) | copy-start | bytes 1572868
  7.2 361.4 %all-reduce.6.cloned.1.call-start = ((), (), s32[]{:S(2)}) async-start(), calls=%async_computation.4 | async-start | bytes 2097152
  58.9 24.3 %copy-start.1 = (f32[16,64,128]{2,1,0:T(8,128)S(1)}, f32[16,64,128]{2,1,0:T(8,128)}, u32[]{:S(2)}) copy-start(f32[16,64,128]{2,1,0:T(8,128)} %param.9) | copy-start | bytes 1572868
  58.9 24.5 %copy-start.3 = (u32[256]{0:T(256)S(1)}, u32[256]{0:T(256)}, u32[]{:S(2)}) copy-start(u32[256]{0:T(256)} %constant.18) | copy-start | bytes 3076
  82.3 344.4 %all-gather.3.cloned.1.call-start = ((), (), s32[]{:S(2)}) async-start(), calls=%async_computation.2 | async-start | bytes 1081344 | tf_op jit(solution)/shard_map/all_gather | solution.py:20
  83.0 638.5 %all-reduce.4.cloned.1.call-start = ((), (), s32[]{:S(2)}) async-start(), calls=%async_computation.1 | async-start | bytes 1048576 | tf_op jit(solution)/shard_map/psum | solution.py:55
  457.4 16.3 %copy-start.2 = (f32[128]{0:T(128)S(1)}, f32[128]{0:T(128)}, u32[]{:S(2)}) copy-start(f32[128]{0:T(128)} %param.8) | copy-start | bytes 1540
  467.3 296.3 %reduce-scatter.5.cloned.1.call-start = ((), (), s32[]{:S(2)}) async-start(), calls=%async_computation.3 | async-start | bytes 294912
Sparse Core Ops, SparseCore 0:
  82.4 286.1 all-reduce.5
  371.1 55.5 all-gather.2
  467.4 254.0 all-reduce.3
  724.4 39.1 reduce-scatter.4
where the time goes:
time: 771 us; the launch traced here: 770 us
  waiting for transfers between devices  533 us (69%)
  blocking collectives  107 us (14%)
  matrix products  57.4 us (7%)
  local copies, waits for them, and re-layouts  55.4 us (7%)
  between operations  14.5 us (2%)
    unnamed x6, waiting for transfers between devices  247 us
    psum x1, waiting for transfers between devices, body(): grad_weight, grad_bias = lax.psum((weight_term, bias_term), ('row', 'col'))  230 us
    psum x1, blocking collectives, body(): grad_weight, grad_bias = lax.psum((weight_term, bias_term), ('row', 'col'))  77.5 us
    all_gather x1, waiting for transfers between devices, body(): right_all = lax.all_gather(right, 'row', axis=0, tiled=True)  55.6 us
    all_gather x1, blocking collectives, body(): left_all = lax.all_gather(left, 'col', axis=0, tiled=True)  29.5 us
    dot_general x1, matrix products, body(): jnp.einsum('icje,cez->ijz', outer_split, weight_cube, precision=highest)  17.6 us
  transfers between devices with their start and end apart: 4, of which 4 were waited for; matrix products, arithmetic and copies ran while one was open for 4% of the time, Pallas kernels for 0%

commit v1 on v0

--- a/solution.py
+++ b/solution.py
@@ -17,7 +17,10 @@
     contract_rows = (((0,), (0,)), ((), ()))
     contract_cols = (((1,), (1,)), ((), ()))
     left_all = lax.all_gather(left, "col", axis=0, tiled=True)
-    right_all = lax.all_gather(right, "row", axis=0, tiled=True)
+    map_tails_up = lambda field_in: jnp.concatenate(
+        lax.all_to_all(jnp.stack(lax.axis_size("row") * [field_in], axis=0), "row", 0, 0), axis=0
+    )
+    right_all = map_tails_up(right)
     outer = (
         lax.dot_general(
             left_all,

time: 771 us -> 734 us (0.952)
  waiting for transfers between devices: 533 us -> 484 us
  starting transfers between devices: 0.56 us -> 12.1 us
    all_gather x1 -> x0, waiting for transfers between devices: 55.6 us -> none  [body(): right_all = lax.all_gather(right, 'row', axis=0, tiled=True)]
    all_to_all x0 -> x1, starting transfers between devices: none -> 11.7 us  [body(): lax.all_to_all(jnp.stack(lax.axis_size('row') * [field_in], axis=0), 'row...]
    unnamed x6 -> x5, waiting for transfers between devices: 247 us -> 248 us
  transfers between devices with their start and end apart: 4 -> 4, of which waited for: 4 -> 3; matrix products, arithmetic and copies ran while one was open for 4% -> 10% of each run, Pallas kernels for 0% -> 0%
where the time goes in v1:
time: 734 us; the launch traced here: 732 us
  waiting for transfers between devices  484 us (66%)
  blocking collectives  104 us (14%)
  matrix products  57.4 us (8%)
  local copies, waits for them, and re-layouts  56.3 us (8%)
  between operations  16.2 us (2%)
  starting transfers between devices  12.1 us (2%)
    unnamed x5, waiting for transfers between devices  248 us
    psum x1, waiting for transfers between devices, body(): grad_weight, grad_bias = lax.psum((weight_term, bias_term), ('row', 'col'))  236 us
    psum x1, blocking collectives, body(): grad_weight, grad_bias = lax.psum((weight_term, bias_term), ('row', 'col'))  75.8 us
    all_gather x1, blocking collectives, body(): left_all = lax.all_gather(left, 'col', axis=0, tiled=True)  28.6 us
    dot_general x1, matrix products, body(): jnp.einsum('icje,cez->ijz', outer_split, weight_cube, precision=highest)  17.6 us
  transfers between devices with their start and end apart: 4, of which 3 were waited for; matrix products, arithmetic and copies ran while one was open for 10% of the time, Pallas kernels for 0%

profile of v1, /device:TPU:8, one launch (start us, length us, event | category | flops | bytes accessed | tf_op | source)
XLA Modules:
  0.0 732.5 jit_solution(11603031145558736444)
XLA Ops:
  8.0 2.1 stack.2
  10.1 11.7 %all-to-all-start = ((f32[32,4,2048]{2,1,0:T(4,128)}), f32[32,4,2048]{2,1,0:T(4,128)S(1)}, u32[]{:S(2)}, u32[]{:S(2)}) async-start(f32[32,4,2048]{2,1,0:T(4,128)} %stack.2), calls=%async_computation | async-start | bytes 2097152 | tf_op jit(solution)/shard_map/all_to_all | solution.py:21
  21.9 9.8 %convolution_bitcast_fusion = f32[16,32,64,32]{2,3,0,1:T(8,128)} fusion(f32[32,32,128,1]{2,1,3,0:T(8,128)S(1)} %bitcast.42, f32[16,64,128]{2,1,0:T(8,128)} %param.9), kind=kOutput, calls=%fused_computation.1 | convolution fusion | flops 1610612736 | bytes 5242880 | tf_op jit(solution)/shard_map/ijz,cez->icje/dot_general | solution.py:36
  31.7 12.3 %copy.21 = f32[16,32,64,32]{3,2,1,0:T(8,128)} copy(f32[16,32,64,32]{2,3,0,1:T(8,128)} %convolution_bitcast_fusion) | data formatting | bytes 8388608 | tf_op jit(solution)/shard_map/ijz,cez->icje/transpose | solution.py:36
  44.0 13.5 %reshape.30 = f32[512,2048]{1,0:T(8,128)} reshape(f32[16,32,64,32]{3,2,1,0:T(8,128)} %copy.21) | data formatting | bytes 8388608 | tf_op jit(solution)/shard_map/reshape | solution.py:37
  57.5 28.6 %all_gather.3 = f32[128,512]{1,0:T(8,128)S(1)} all-gather(f32[16,512]{1,0:T(8,128)S(1)} %copy-done.2), channel_id=1, replica_groups=mesh['row'=32,'col'=8] {'col'}, dimensions={0}, use_global_device_ids=true | all-gather | bytes 294912 | tf_op jit(solution)/shard_map/all_gather | solution.py:19
  86.1 9.9 %fusion = f32[128,2048]{0,1:T(8,128)} fusion(f32[512,2048]{1,0:T(8,128)} %reshape.30, f32[128,512]{1,0:T(8,128)S(1)} %all_gather.3), kind=kOutput, calls=%fused_computation.3 | convolution fusion | flops 1610874880 | bytes 5505024 | tf_op jit(solution)/shard_map/dot_general | solution.py:52
  96.2 0.6 dynamic-slice
  97.4 75.8 %psum.15 = f32[128]{0:T(128)S(1)} all-reduce(f32[128]{0:T(128)S(1)} %reduce_sum.9), channel_id=1, replica_groups=mesh['row'=32,'col'=8] {'row','col'}, use_global_device_ids=true, to_apply=%region_4.0 | all-reduce | flops 128 | bytes 1024 | tf_op jit(solution)/shard_map/psum | solution.py:58
  173.2 0.5 broadcast_multiply_fusion.1
  173.7 207.5 %all-reduce.6.cloned.1.call-done = f32[128,2048]{0,1:T(8,128)} async-done(((f32[128,2048]{0,1:T(8,128)}), f32[128,2048]{0,1:T(8,128)}) %all-reduce.6.cloned.1.call-update) | async-done | bytes 1048592
  381.3 1.6 constant_dynamic-slice_fusion
  382.8 0.9 copy.25
  383.8 0.4 reshape.27
  384.1 5.0 convolution_multiply_fusion
  389.2 11.4 %reshape.28 = f32[16,32,64,32]{3,2,1,0:T(8,128)} reshape(f32[512,2048]{1,0:T(8,128)} %convolution_multiply_fusion) | data formatting | bytes 8388608 | tf_op jit(solution)/shard_map/reshape | solution.py:34
  400.6 12.7 %copy.33 = f32[32,32,16,64]{3,1,0,2:T(8,128)} copy(f32[32,32,16,64]{1,3,0,2:T(8,128)} %bitcast.43) | data formatting | bytes 8388608 | tf_op jit(solution)/shard_map/icje,ijz->cez/dot_general | solution.py:54
  413.3 9.9 %convolution_bitcast_fusion.2 = f32[1024,128]{1,0:T(8,128)} fusion(f32[1024,16,64]{2,0,1:T(8,128)} %bitcast.44, f32[16,64,128]{2,1,0:T(8,128)S(1)} %copy-done.1), kind=kOutput, calls=%fused_computation.5 | convolution fusion | flops 1610612736 | bytes 5242880 | tf_op jit(solution)/shard_map/icje,ijz->cez/dot_general | solution.py:54
  423.5 5.2 fusion.2
  428.7 0.8 copy.29
  429.6 17.6 %fusion.1 = f32[16,64,128]{2,1,0:T(8,128)} fusion(f32[16,32,64,32]{3,2,1,0:T(8,128)} %reshape.28, f32[32,32,128,1]{2,1,0,3:T(8,128)S(1)} %bitcast.41, f32[128]{0:T(128)S(1)} %copy-done.3), kind=kOutput, calls=%fused_computation.6 | convolution fusion | flops 1610743808 | bytes 5243392 | tf_op jit(solution)/shard_map/icje,cez->ijz/dot_general | solution.py:35
  447.2 235.7 %all-reduce.4.cloned.1.call-done = f32[1024,128]{1,0:T(8,128)} async-done(((f32[1024,128]{1,0:T(8,128)}), f32[1024,128]{1,0:T(8,128)}) %all-reduce.4.cloned.1.call-update) | async-done | bytes 524304 | tf_op jit(solution)/shard_map/psum | solution.py:58
  682.9 1.9 broadcast_multiply_fusion
  684.7 40.3 %reduce-scatter.5.cloned.1.call-done = f32[16,512]{1,0:T(8,128)} async-done(((f32[128,512]{1,0:T(8,128)}), f32[16,512]{1,0:T(8,128)}) %reduce-scatter.5.cloned.1.call-update) | async-done | bytes 32784
  (18 shorter events, 0.6 us)
Async XLA Ops:
  8.0 13.9 %copy-start = (f32[1024,128]{1,0:T(8,128)S(1)}, f32[1024,128]{1,0:T(8,128)}, u32[]{:S(2)}) copy-start(f32[1024,128]{1,0:T(8,128)} %param.7) | copy-start | bytes 1572868
  10.1 373.7 %all-to-all-start = ((f32[32,4,2048]{2,1,0:T(4,128)}), f32[32,4,2048]{2,1,0:T(4,128)S(1)}, u32[]{:S(2)}, u32[]{:S(2)}) async-start(f32[32,4,2048]{2,1,0:T(4,128)} %stack.2), calls=%async_computation | async-start | bytes 2097152 | tf_op jit(solution)/shard_map/all_to_all | solution.py:21
  21.8 359.5 %all-reduce.6.cloned.1.call-start = ((), (), s32[]{:S(2)}) async-start(), calls=%async_computation.4 | async-start | bytes 2097152
  44.0 13.5 %copy-start.2 = (f32[16,512]{1,0:T(8,128)S(1)}, f32[16,512]{1,0:T(8,128)}, u32[]{:S(2)}) copy-start(f32[16,512]{1,0:T(8,128)} %param.5) | copy-start | bytes 98308
  44.0 52.0 %copy-start.1 = (f32[16,64,128]{2,1,0:T(8,128)S(1)}, f32[16,64,128]{2,1,0:T(8,128)}, u32[]{:S(2)}) copy-start(f32[16,64,128]{2,1,0:T(8,128)} %param.9) | copy-start | bytes 1572868
  44.0 52.2 %copy-start.4 = (u32[256]{0:T(256)S(1)}, u32[256]{0:T(256)}, u32[]{:S(2)}) copy-start(u32[256]{0:T(256)} %constant.18) | copy-start | bytes 3076
  96.0 586.9 %all-reduce.4.cloned.1.call-start = ((), (), s32[]{:S(2)}) async-start(), calls=%async_computation.2 | async-start | bytes 1048576 | tf_op jit(solution)/shard_map/psum | solution.py:58
  413.3 16.3 %copy-start.3 = (f32[128]{0:T(128)S(1)}, f32[128]{0:T(128)}, u32[]{:S(2)}) copy-start(f32[128]{0:T(128)} %param.8) | copy-start | bytes 1540
  423.2 301.8 %reduce-scatter.5.cloned.1.call-start = ((), (), s32[]{:S(2)}) async-start(), calls=%async_computation.3 | async-start | bytes 294912
Sparse Core Ops, SparseCore 0:
  96.1 285.1 all-reduce.5
Sparse Core Ops, SparseCore 1:
  423.3 259.5 all-reduce.3
  685.8 39.2 reduce-scatter.4
